TPU v7x, 512 devices: a whole 4x4x16 slice. The times are simulated.
512 devices in a mesh: expert: 4 (over z_hi, core), rep: 4 (over y), hid: 32 (over x, z_lo).
Axes of the slice: x: 4, y: 4, z: 16 (z_hi: 2, z_lo: 8; z = z_hi * 8 + z_lo), core: 2. Of those that a mesh axis runs over, the one named last changes fastest.
Arguments:
- tokens: bfloat16 [1024, 6144], P(('expert', 'hid'), 'rep'), may hold values from -6 to 6
- norm_gain: float32 [6144], P('rep'), may hold values from 0.25 to 1.75
- expert_ids: int32 [1024, 2], P(('expert', 'hid')), may hold values from 0 to 3, as said below
- slot_ids: int32 [1024, 2], P(('expert', 'hid')), may hold values from 0 to 4, as said below
- w_gate: bfloat16 [4, 6144, 8192], P('expert', 'rep', 'hid'), may hold values from -0.078125 to 0.078125
- w_up: bfloat16 [4, 6144, 8192], P('expert', 'rep', 'hid'), may hold values from -0.078125 to 0.078125
- grad_gate: bfloat16 [4, 640, 8192], P('expert', None, 'hid'), may hold values from -1.1953125 to 1.1953125
- grad_up: bfloat16 [4, 640, 8192], P('expert', None, 'hid'), may hold values from -1.1953125 to 1.1953125
Outputs:
- grad_w_gate: bfloat16 [4, 6144, 8192], P('expert', 'rep', 'hid')
- grad_w_up: bfloat16 [4, 6144, 8192], P('expert', 'rep', 'hid')
- grad_tokens: bfloat16 [1024, 6144], P(('expert', 'hid'), 'rep')
Inputs may be any that keep to these rules, and one draw needn't show every extreme that they name: `expert_ids`: each token names two different experts; among the 8 tokens of one block, no expert is named more than 5 times and some expert exactly 5 times. Within one block of 8 tokens, the pairs (expert_ids[t, k], slot_ids[t, k]) are all different.
All inputs are finite; a program needn't handle non-finite values.
Results may differ from a plain program's by a relative error of at most 0.0049.
Values may be sent and summed in bfloat16 or wider, within the bound.
No kernel may reach another device: no remote copies, remote signals or barrier semaphores. Data moves between devices by JAX's collectives and lax.ppermute only.
A program may use at most 64 MiB of HBM per device.

v0:
```python
import jax
import jax.numpy as jnp
from jax import lax
from jax.sharding import Mesh
from jax.sharding import PartitionSpec as P


D = 6144
CAP = 5
TOK = 8
RING = ("zh", "zl")
LANES = 128


def exchange(x, axis):
    return lax.all_to_all(x, axis, 0, 0, tiled=True)


def copy_for_each(x, axis):
    size = lax.axis_size(axis)
    return exchange(jnp.broadcast_to(x[None], (size, *x.shape)), axis)


def feature_total(partial_value):
    return copy_for_each(partial_value[None], "rep").sum(axis=(0, 1))


def along_x(x, step):
    size = lax.axis_size("x")
    return lax.ppermute(x, "x", [(i, (i + step) % size) for i in range(size)])


def swap_cores(x):
    return lax.ppermute(x, "core", [(0, 1), (1, 0)])


def on_device(tokens, norm_gain, expert_ids, slot_ids, w_gate, w_up, grad_gate, grad_up):
    zh_n, core_n, x_n, zl_n = (lax.axis_size(a) for a in ("zh", "core", "x", "zl"))
    ring_n = zh_n * zl_n
    line_tokens = ring_n * TOK
    line_rows = zl_n * zh_n * core_n * CAP
    width = tokens.shape[1]
    core = lax.axis_index("core")
    mine = lax.axis_index("zh") * core_n + core
    partner = lax.axis_index("zh") * core_n + (1 - core)

    unit_contract = (((1,), (1,)), ((), ()))
    here = lax.axis_index("x")

    def part_for(step):
        at = lax.rem(here + step, x_n) * line_rows
        gate = lax.dynamic_slice_in_dim(grad_gate[0], at, line_rows)
        up = lax.dynamic_slice_in_dim(grad_up[0], at, line_rows)
        return lax.dot_general(
            gate, w_gate[0], unit_contract, preferred_element_type=jnp.float32
        ) + lax.dot_general(up, w_up[0], unit_contract, preferred_element_type=jnp.float32)

    arriving = []
    for step in (2, 1, 3):
        piece = part_for(step).astype(jnp.bfloat16)
        arriving.append(along_x(piece, step).astype(jnp.float32))

    values = tokens.astype(jnp.float32)
    square_sums = feature_total(jnp.sum(values * values, axis=1))
    inverse_rms = lax.rsqrt(square_sums / D + 1e-05)[:, None]
    scaled_in = values * inverse_rms
    normed = (scaled_in * norm_gain).astype(jnp.bfloat16)
    code = (expert_ids * CAP + slot_ids).astype(jnp.bfloat16)
    tagged = jnp.concatenate([normed, jnp.pad(code, ((0, 0), (0, LANES - 2)))], axis=1)

    line = copy_for_each(tagged, RING).reshape(line_tokens, width + LANES)
    line_normed = line[:, :width]
    codes = line[:, width : width + 2].astype(jnp.int32)
    token = jnp.arange(line_tokens, dtype=jnp.int32)
    block = token // TOK
    base = (((block % zl_n) * zh_n + block // zl_n) * core_n + core) * CAP

    def rows_of(expert):
        slot = codes - expert * CAP
        return jnp.where((slot >= 0) & (slot < CAP), base[:, None] + slot, -1)

    row = jnp.arange(line_rows, dtype=jnp.int32)

    def choice(expert):
        at = rows_of(expert)
        return ((at[:, 0][:, None] == row[None]) | (at[:, 1][:, None] == row[None])).astype(
            jnp.bfloat16
        )

    to_mine = choice(mine)
    to_partner = choice(partner)
    first = (((0,), (0,)), ((), ()))

    def rows_from(chosen):
        return lax.dot_general(
            chosen, line_normed, first, preferred_element_type=jnp.float32
        ).astype(jnp.bfloat16)

    for_partner = rows_from(to_partner)
    from_partner = swap_cores(for_partner)
    own_rows = rows_from(to_mine) + from_partner
    steps = (0, 1, 3, 2)
    gathered = jnp.concatenate([own_rows] + [along_x(own_rows, step) for step in steps[1:]])

    def in_order(cotangent):
        return jnp.concatenate(
            [
                lax.dynamic_slice_in_dim(
                    cotangent, lax.rem(here - step + x_n, x_n) * line_rows, line_rows
                )
                for step in steps
            ]
        )

    new_gate = lax.dot_general(
        gathered, in_order(grad_gate[0]), first, preferred_element_type=jnp.float32
    )
    new_up = lax.dot_general(
        gathered, in_order(grad_up[0]), first, preferred_element_type=jnp.float32
    )

    line_sum = (part_for(0) + arriving[0] + arriving[1] + arriving[2]).astype(jnp.bfloat16)
    other_sum = swap_cores(line_sum)
    by_token = jnp.dot(to_mine, line_sum, preferred_element_type=jnp.float32) + jnp.dot(
        to_partner, other_sum, preferred_element_type=jnp.float32
    )
    by_token = by_token.astype(jnp.bfloat16).reshape(ring_n, TOK, width)
    normed_grad = exchange(by_token, RING).astype(jnp.float32).sum(axis=0)

    scaled = normed_grad * norm_gain
    partial_dots = jnp.sum(scaled * scaled_in, axis=1)
    dotted = feature_total(partial_dots) / D
    grad_tokens = (inverse_rms * (scaled - scaled_in * dotted[:, None])).astype(jnp.bfloat16)
    return (new_gate.astype(jnp.bfloat16)[None], new_up.astype(jnp.bfloat16)[None], grad_tokens)


def solution(mesh):
    physical = Mesh(mesh.devices.reshape(2, 2, 4, 4, 8), ("zh", "core", "rep", "x", "zl"))
    expert, hid = ("zh", "core"), ("x", "zl")
    placed = (
        P(expert + hid, "rep"),
        P("rep"),
        P(expert + hid, None),
        P(expert + hid, None),
        P(expert, "rep", hid),
        P(expert, "rep", hid),
        P(expert, None, hid),
        P(expert, None, hid),
    )

    return jax.shard_map(
        on_device,
        mesh=physical,
        in_specs=placed,
        out_specs=(P(expert, "rep", hid), P(expert, "rep", hid), P(expert + hid, "rep")),
        check_vma=False,
    )
```

profile of v0, /device:TPU:2, one launch (start us, length us, event | category | flops | bytes accessed | tf_op | source)
XLA Modules:
  0.0 120.3 jit_solution(7220316968498490810)
XLA Ops:
  0.7 2.0 %dynamic-slice_bitcast_fusion.3 = (bf16[160,256]{1,0:T(8,128)(2,1)}, bf16[160,256]{1,0:T(8,128)(2,1)}, bf16[160,256]{1,0:T(8,128)(2,1)}, bf16[160,256]{1,0:T(8,1...) fusion(bf16[1,640,256]{2,1,0:T(8,128)(2,1)} %param.15, ...), kind=kLoop, calls=%fused_computation.70 | loop fusion | bytes 1310736 | tf_op jit(solution)/shard_map/dynamic_slice | solution.py:108
  2.7 0.4 fusion.18
  3.1 0.2 copy-done.3
  3.3 0.6 copy-done.1
  3.9 1.2 fusion.2
  5.1 4.2 %collective-permute-start.4 = (bf16[160,1536]{1,0:T(8,128)(2,1)}, bf16[160,1536]{1,0:T(8,128)(2,1)S(1)}, u32[]{:S(2)}, u32[]{:S(2)}) collective-permute-start(bf16[160,1536]{1,0:T(8,128)(2,1)} %fusion.2), channel_id=1, source_target_pairs={{0,16},{8,24},{16,0},{24,8},{1,17},{9,25},{17,1},{25,9},{2,18},{10... | collective-permute-start | bytes 1474568 | tf_op jit(solution)/shard_map/ppermute | solution.py:30
  9.3 0.1 fusion.76
  9.4 0.6 broadcast_in_dim.15
  10.0 4.5 %all-to-all-start = ((f32[4,1,8]{2,1,0:T(1,128)}), f32[4,1,8]{2,1,0:T(1,128)S(1)}, u32[]{:S(2)}, u32[]{:S(2)}) async-start(f32[4,1,8]{2,1,0:T(1,128)} %broadcast_in_dim.15), calls=%async_computation | async-start | bytes 4096 | tf_op jit(solution)/shard_map/all_to_all | solution.py:16
  14.5 0.4 fusion.16
  14.9 0.1 copy.21
  15.0 0.1 copy.22
  15.1 4.6 %all-to-all-done = f32[4,1,8]{2,1,0:T(1,128)S(1)} async-done(((f32[4,1,8]{2,1,0:T(1,128)}), f32[4,1,8]{2,1,0:T(1,128)S(1)}, u32[]{:S(2)}, u32[]{:S(2)}) %all-to-all-start) | async-done | bytes 160 | tf_op jit(solution)/shard_map/all_to_all | solution.py:16
  19.8 0.8 broadcast_in_dim.16
  20.6 15.2 %all-to-all-start.1 = ((bf16[16,8,1664]{2,1,0:T(8,128)(2,1)}), bf16[16,8,1664]{2,1,0:T(8,128)(2,1)S(1)}, u32[]{:S(2)}, u32[]{:S(2)}) async-start(bf16[16,8,1664]{2,1,0:T(8,128)(2,1)} %broadcast_in_dim.16), calls=%async_computation.1 | async-start | bytes 851968 | tf_op jit(solution)/shard_map/all_to_all | solution.py:16
  35.8 2.1 %fusion.3 = bf16[160,1536]{1,0:T(8,128)(2,1)} fusion(f32[160,1536]{1,0:T(8,128)S(1)} %fusion.16, bf16[160,256]{1,0:T(8,128)(2,1)} %get-tuple-element.10, bf16[1,1536,256]{2,1,0:T(8,128)(2,1)S(1)} %copy-done.1), kind=kOutput, calls=%fused_computation.10 | convolution fusion | flops 126320640 | bytes 2342912 | tf_op jit(solution)/shard_map/dot_general | solution.py:56
  37.9 2.0 %collective-permute-start.5 = (bf16[160,1536]{1,0:T(8,128)(2,1)}, bf16[160,1536]{1,0:T(8,128)(2,1)S(1)}, u32[]{:S(2)}, u32[]{:S(2)}) collective-permute-start(bf16[160,1536]{1,0:T(8,128)(2,1)} %fusion.3), channel_id=1, source_target_pairs={{0,8},{8,16},{16,24},{24,0},{1,9},{9,17},{17,25},{25,1},{2,10},{10... | collective-permute-start | bytes 1474568 | tf_op jit(solution)/shard_map/ppermute | solution.py:30
  40.0 0.4 fusion.14
  40.4 0.4 fusion.4
  40.8 3.9 %collective-permute-start.6 = (bf16[160,1536]{1,0:T(8,128)(2,1)S(1)}, bf16[160,1536]{1,0:T(8,128)(2,1)}, u32[]{:S(2)}, u32[]{:S(2)}) collective-permute-start(bf16[160,1536]{1,0:T(8,128)(2,1)S(1)} %fusion.4), channel_id=1, source_target_pairs={{0,24},{8,0},{16,8},{24,16},{1,25},{9,1},{17,9},{25,17},{2,26},{10... | collective-permute-start | bytes 1474568 | tf_op jit(solution)/shard_map/ppermute | solution.py:30
  44.8 1.3 %fusion.20 = f32[160,1536]{1,0:T(8,128)S(1)} fusion(bf16[1,1536,256]{2,1,0:T(8,128)(2,1)S(1)} %copy-done, bf16[1,640,256]{2,1,0:T(8,128)(2,1)} %param.14, s32[]{:T(128)S(6)} %select_n.69), kind=kOutput, calls=%fused_computation.29 | convolution fusion | flops 125829120 | bytes 1851396 | tf_op jit(solution)/shard_map/dot_general | solution.py:54
  46.1 5.0 %collective-permute-done.5 = bf16[160,1536]{1,0:T(8,128)(2,1)S(1)} collective-permute-done((bf16[160,1536]{1,0:T(8,128)(2,1)}, bf16[160,1536]{1,0:T(8,128)(2,1)S(1)}, u32[]{:S(2)}, u32[]{:S(2)}) %collective-permute-start.5) | collective-permute-done | bytes 491552 | tf_op jit(solution)/shard_map/ppermute | solution.py:30
  51.1 2.9 %collective-permute-done.6 = bf16[160,1536]{1,0:T(8,128)(2,1)} collective-permute-done((bf16[160,1536]{1,0:T(8,128)(2,1)S(1)}, bf16[160,1536]{1,0:T(8,128)(2,1)}, u32[]{:S(2)}, u32[]{:S(2)}) %collective-permute-start.6) | collective-permute-done | bytes 491552 | tf_op jit(solution)/shard_map/ppermute | solution.py:30
  54.0 1.6 %add_convert_fusion = bf16[160,1536]{1,0:T(8,128)(2,1)S(1)} fusion(bf16[160,1536]{1,0:T(8,128)(2,1)} %collective-permute-done.6, bf16[160,1536]{1,0:T(8,128)(2,1)S(1)} %collective-permute-done.5, bf16[160,1536]{1,0:T(8,128)(2,1)S(1)} %collective-permute-done.4, f32[160,1536]{1,0:T(8,128)S(1)} %fusion.20, bf16[1,1536,256]{2,1,0:T(8,128)(2,1)S(1)} %copy-done.1, ...), kind=kOutput, calls=%fused_computation.18 | convolution fusion | flops 127795200 | bytes 3817476 | tf_op jit(solution)/shard_map/dot_general | solution.py:56
  55.6 1.9 %collective-permute-start.7 = (bf16[160,1536]{1,0:T(8,128)(2,1)S(1)}, bf16[160,1536]{1,0:T(8,128)(2,1)S(1)}, u32[]{:S(2)}, u32[]{:S(2)}) collective-permute-start(bf16[160,1536]{1,0:T(8,128)(2,1)S(1)} %add_convert_fusion), channel_id=1, source_target_pairs={{0,128},{128,0},{1,129},{129,1},{2,130},{130,2},{3,131},{131,3},{4... | collective-permute-start | bytes 1474568 | tf_op jit(solution)/shard_map/ppermute | solution.py:34
  57.5 0.9 all-to-all-done.1
  58.4 0.1 fusion.56
  58.5 0.2 slice_reduce_fusion.1
  58.7 1.2 convolution_convert_fusion.2
  59.9 1.9 %collective-permute-start = (bf16[160,1536]{1,0:T(8,128)(2,1)}, bf16[160,1536]{1,0:T(8,128)(2,1)}, u32[]{:S(2)}, u32[]{:S(2)}) collective-permute-start(bf16[160,1536]{1,0:T(8,128)(2,1)} %convolution_convert_fusion.2), channel_id=1, source_target_pairs={{0,128},{128,0},{1,129},{129,1},{2,130},{130,2},{3,131},{131,3},{4... | collective-permute-start | bytes 1474568 | tf_op jit(solution)/shard_map/ppermute | solution.py:34
  61.8 0.2 slice_reduce_fusion.3
  62.0 0.3 fusion.40
  62.3 1.1 fusion.7
  63.4 11.5 %all-to-all-start.2 = ((bf16[16,8,1536]{2,1,0:T(8,128)(2,1)}), bf16[16,8,1536]{2,1,0:T(8,128)(2,1)S(1)}, u32[]{:S(2)}, u32[]{:S(2)}) async-start(bf16[16,8,1536]{2,1,0:T(8,128)(2,1)} %fusion.7), calls=%async_computation.2 | async-start | bytes 786432 | tf_op jit(solution)/shard_map/all_to_all | solution.py:16
  74.9 1.4 %fusion.6 = bf16[160,1536]{1,0:T(8,128)(2,1)S(1)} fusion(bf16[160,1536]{1,0:T(8,128)(2,1)} %collective-permute-done, bf16[128,1664]{1,0:T(8,128)(2,1)S(1)} %bitcast.61, s32[128]{0:T(128)S(1)} %get-tuple-element.4, s32[128]{0:T(128)S(1)} %get-tuple-element.3), kind=kOutput, calls=%fused_computation.15 | convolution fusion | flops 63467520 | bytes 1377280 | tf_op jit(solution)/shard_map/dot_general | solution.py:95
  76.4 4.0 %collective-permute-start.1 = (bf16[160,1536]{1,0:T(8,128)(2,1)S(1)}, bf16[160,1536]{1,0:T(8,128)(2,1)S(1)}, u32[]{:S(2)}, u32[]{:S(2)}) collective-permute-start(bf16[160,1536]{1,0:T(8,128)(2,1)S(1)} %fusion.6), channel_id=1, source_target_pairs={{0,8},{8,16},{16,24},{24,0},{1,9},{9,17},{17,25},{25,1},{2,10},{10... | collective-permute-start | bytes 1474568 | tf_op jit(solution)/shard_map/ppermute | solution.py:30
  80.4 1.9 %collective-permute-start.2 = (bf16[160,1536]{1,0:T(8,128)(2,1)S(1)}, bf16[160,1536]{1,0:T(8,128)(2,1)S(1)}, u32[]{:S(2)}, u32[]{:S(2)}) collective-permute-start(bf16[160,1536]{1,0:T(8,128)(2,1)S(1)} %fusion.6), channel_id=1, source_target_pairs={{0,24},{8,0},{16,8},{24,16},{1,25},{9,1},{17,9},{25,17},{2,26},{10... | collective-permute-start | bytes 1474568 | tf_op jit(solution)/shard_map/ppermute | solution.py:30
  82.3 6.3 %collective-permute-start.3 = (bf16[160,1536]{1,0:T(8,128)(2,1)S(1)}, bf16[160,1536]{1,0:T(8,128)(2,1)S(1)}, u32[]{:S(2)}, u32[]{:S(2)}) collective-permute-start(bf16[160,1536]{1,0:T(8,128)(2,1)S(1)} %fusion.6), channel_id=1, source_target_pairs={{0,16},{8,24},{16,0},{24,8},{1,17},{9,25},{17,1},{25,9},{2,18},{10... | collective-permute-start | bytes 1474568 | tf_op jit(solution)/shard_map/ppermute | solution.py:30
  88.6 12.7 %collective-permute-done.1 = bf16[160,1536]{1,0:T(8,128)(2,1)S(1)} collective-permute-done((bf16[160,1536]{1,0:T(8,128)(2,1)S(1)}, bf16[160,1536]{1,0:T(8,128)(2,1)S(1)}, u32[]{:S(2)}, u32[]{:S(2)}) %collective-permute-start.1) | collective-permute-done | bytes 491552 | tf_op jit(solution)/shard_map/ppermute | solution.py:30
  101.3 6.5 %collective-permute-done.3 = bf16[160,1536]{1,0:T(8,128)(2,1)S(1)} collective-permute-done((bf16[160,1536]{1,0:T(8,128)(2,1)S(1)}, bf16[160,1536]{1,0:T(8,128)(2,1)S(1)}, u32[]{:S(2)}, u32[]{:S(2)}) %collective-permute-start.3) | collective-permute-done | bytes 491552 | tf_op jit(solution)/shard_map/ppermute | solution.py:30
  107.8 0.8 copy-done.19
  108.6 1.7 %fusion.1 = bf16[1,1536,256]{2,1,0:T(8,128)(2,1)} fusion(bf16[160,1536]{1,0:T(8,128)(2,1)S(1)} %collective-permute-done.3, bf16[160,1536]{1,0:T(8,128)(2,1)S(1)} %collective-permute-done.2, bf16[160,1536]{1,0:T(8,128)(2,1)S(1)} %collective-permute-done.1, bf16[160,1536]{1,0:T(8,128)(2,1)S(1)} %fusion.6, bf16[160,256]{1,0:T(8,128)(2,1)S(1)} %copy-done.13, ...), kind=kOutput, calls=%fused_computation.8 | convolution fusion | flops 512884736 | bytes 3080192 | tf_op jit(solution)/shard_map/dot_general | solution.py:118
  110.4 0.2 fusion.72
  110.6 0.6 broadcast_in_dim.20
  111.1 3.2 %all-to-all-start.3 = ((f32[4,1,8]{2,1,0:T(1,128)}), f32[4,1,8]{2,1,0:T(1,128)S(1)}, u32[]{:S(2)}, u32[]{:S(2)}) async-start(f32[4,1,8]{2,1,0:T(1,128)} %broadcast_in_dim.20), calls=%async_computation.3 | async-start | bytes 4096 | tf_op jit(solution)/shard_map/all_to_all | solution.py:16
  114.4 2.7 %fusion = bf16[1,1536,256]{2,1,0:T(8,128)(2,1)} fusion(bf16[160,1536]{1,0:T(8,128)(2,1)} %copy-done.19, bf16[160,1536]{1,0:T(8,128)(2,1)S(1)} %collective-permute-done.2, bf16[160,1536]{1,0:T(8,128)(2,1)S(1)} %collective-permute-done.1, bf16[160,1536]{1,0:T(8,128)(2,1)S(1)} %fusion.6, bf16[160,256]{1,0:T(8,128)(2,1)S(1)} %copy-done.4, ...), kind=kOutput, calls=%fused_computation.7 | convolution fusion | flops 512884736 | bytes 3080192 | tf_op jit(solution)/shard_map/dot_general | solution.py:115
  117.2 2.4 %all-to-all-done.3 = f32[4,1,8]{2,1,0:T(1,128)S(1)} async-done(((f32[4,1,8]{2,1,0:T(1,128)}), f32[4,1,8]{2,1,0:T(1,128)S(1)}, u32[]{:S(2)}, u32[]{:S(2)}) %all-to-all-start.3) | async-done | bytes 160 | tf_op jit(solution)/shard_map/all_to_all | solution.py:16
  119.6 0.7 fusion.75
  (51 shorter events, 0.3 us)
Async XLA Ops:
  0.6 2.1 %copy-start = (bf16[1,1536,256]{2,1,0:T(8,128)(2,1)S(1)}, bf16[1,1536,256]{2,1,0:T(8,128)(2,1)}, u32[]{:S(2)}) copy-start(bf16[1,1536,256]{2,1,0:T(8,128)(2,1)} %param.12) | copy-start | bytes 2359300
  2.7 0.6 copy-start.3
  2.7 2.4 %copy-start.12 = (bf16[160,256]{1,0:T(8,128)(2,1)}, bf16[160,256]{1,0:T(8,128)(2,1)S(1)}, u32[]{:S(2)}) copy-start(bf16[160,256]{1,0:T(8,128)(2,1)S(1)} %get-tuple-element.12) | copy-start | bytes 245764
  2.7 11.8 %copy-start.7 = (bf16[160,256]{1,0:T(8,128)(2,1)}, bf16[160,256]{1,0:T(8,128)(2,1)S(1)}, u32[]{:S(2)}) copy-start(bf16[160,256]{1,0:T(8,128)(2,1)S(1)} %get-tuple-element.19) | copy-start | bytes 245764
  2.7 1.2 %copy-start.1 = (bf16[1,1536,256]{2,1,0:T(8,128)(2,1)S(1)}, bf16[1,1536,256]{2,1,0:T(8,128)(2,1)}, u32[]{:S(2)}) copy-start(bf16[1,1536,256]{2,1,0:T(8,128)(2,1)} %param.13) | copy-start | bytes 2359300
  3.9 5.4 %copy-start.2 = (bf16[8,1536]{1,0:T(8,128)(2,1)S(1)}, bf16[8,1536]{1,0:T(8,128)(2,1)}, u32[]{:S(2)}) copy-start(bf16[8,1536]{1,0:T(8,128)(2,1)} %param.8) | copy-start | bytes 73732
  5.1 9.8 %copy-start.17 = (s32[8,2]{0,1:T(2,128)S(1)}, s32[8,2]{0,1:T(2,128)}, u32[]{:S(2)}) copy-start(s32[8,2]{0,1:T(2,128)} %param.10) | copy-start | bytes 196
  5.1 9.9 %copy-start.18 = (s32[8,2]{0,1:T(2,128)S(1)}, s32[8,2]{0,1:T(2,128)}, u32[]{:S(2)}) copy-start(s32[8,2]{0,1:T(2,128)} %param.11) | copy-start | bytes 196
  5.1 14.6 %copy-start.16 = (f32[1536]{0:T(1024)S(1)}, f32[1536]{0:T(1024)}, u32[]{:S(2)}) copy-start(f32[1536]{0:T(1024)} %param.9) | copy-start | bytes 18436
  5.1 41.0 %collective-permute-start.4 = (bf16[160,1536]{1,0:T(8,128)(2,1)}, bf16[160,1536]{1,0:T(8,128)(2,1)S(1)}, u32[]{:S(2)}, u32[]{:S(2)}) collective-permute-start(bf16[160,1536]{1,0:T(8,128)(2,1)} %fusion.2), channel_id=1, source_target_pairs={{0,16},{8,24},{16,0},{24,8},{1,17},{9,25},{17,1},{25,9},{2,18},{10... | collective-permute-start | bytes 1474568 | tf_op jit(solution)/shard_map/ppermute | solution.py:30
  10.0 9.7 %all-to-all-start = ((f32[4,1,8]{2,1,0:T(1,128)}), f32[4,1,8]{2,1,0:T(1,128)S(1)}, u32[]{:S(2)}, u32[]{:S(2)}) async-start(f32[4,1,8]{2,1,0:T(1,128)} %broadcast_in_dim.15), calls=%async_computation | async-start | bytes 4096 | tf_op jit(solution)/shard_map/all_to_all | solution.py:16
  20.6 37.8 %all-to-all-start.1 = ((bf16[16,8,1664]{2,1,0:T(8,128)(2,1)}), bf16[16,8,1664]{2,1,0:T(8,128)(2,1)S(1)}, u32[]{:S(2)}, u32[]{:S(2)}) async-start(bf16[16,8,1664]{2,1,0:T(8,128)(2,1)} %broadcast_in_dim.16), calls=%async_computation.1 | async-start | bytes 851968 | tf_op jit(solution)/shard_map/all_to_all | solution.py:16
  35.8 4.2 %copy-start.5 = (bf16[160,256]{1,0:T(8,128)(2,1)S(1)}, bf16[160,256]{1,0:T(8,128)(2,1)}, u32[]{:S(2)}) copy-start(bf16[160,256]{1,0:T(8,128)(2,1)} %get-tuple-element.18) | copy-start | bytes 245764
  37.9 2.5 %copy-start.10 = (bf16[160,256]{1,0:T(8,128)(2,1)S(1)}, bf16[160,256]{1,0:T(8,128)(2,1)}, u32[]{:S(2)}) copy-start(bf16[160,256]{1,0:T(8,128)(2,1)} %get-tuple-element.11) | copy-start | bytes 245764
  37.9 13.2 %collective-permute-start.5 = (bf16[160,1536]{1,0:T(8,128)(2,1)}, bf16[160,1536]{1,0:T(8,128)(2,1)S(1)}, u32[]{:S(2)}, u32[]{:S(2)}) collective-permute-start(bf16[160,1536]{1,0:T(8,128)(2,1)} %fusion.3), channel_id=1, source_target_pairs={{0,8},{8,16},{16,24},{24,0},{1,9},{9,17},{17,25},{25,1},{2,10},{10... | collective-permute-start | bytes 1474568 | tf_op jit(solution)/shard_map/ppermute | solution.py:30
  40.8 13.2 %collective-permute-start.6 = (bf16[160,1536]{1,0:T(8,128)(2,1)S(1)}, bf16[160,1536]{1,0:T(8,128)(2,1)}, u32[]{:S(2)}, u32[]{:S(2)}) collective-permute-start(bf16[160,1536]{1,0:T(8,128)(2,1)S(1)} %fusion.4), channel_id=1, source_target_pairs={{0,24},{8,0},{16,8},{24,16},{1,25},{9,1},{17,9},{25,17},{2,26},{10... | collective-permute-start | bytes 1474568 | tf_op jit(solution)/shard_map/ppermute | solution.py:30
  55.6 6.4 %collective-permute-start.7 = (bf16[160,1536]{1,0:T(8,128)(2,1)S(1)}, bf16[160,1536]{1,0:T(8,128)(2,1)S(1)}, u32[]{:S(2)}, u32[]{:S(2)}) collective-permute-start(bf16[160,1536]{1,0:T(8,128)(2,1)S(1)} %add_convert_fusion), channel_id=1, source_target_pairs={{0,128},{128,0},{1,129},{129,1},{2,130},{130,2},{3,131},{131,3},{4... | collective-permute-start | bytes 1474568 | tf_op jit(solution)/shard_map/ppermute | solution.py:34
  59.9 15.0 %collective-permute-start = (bf16[160,1536]{1,0:T(8,128)(2,1)}, bf16[160,1536]{1,0:T(8,128)(2,1)}, u32[]{:S(2)}, u32[]{:S(2)}) collective-permute-start(bf16[160,1536]{1,0:T(8,128)(2,1)} %convolution_convert_fusion.2), channel_id=1, source_target_pairs={{0,128},{128,0},{1,129},{129,1},{2,130},{130,2},{3,131},{131,3},{4... | collective-permute-start | bytes 1474568 | tf_op jit(solution)/shard_map/ppermute | solution.py:34
  63.4 45.2 %copy-start.9 = (bf16[160,256]{1,0:T(8,128)(2,1)S(1)}, bf16[160,256]{1,0:T(8,128)(2,1)}, u32[]{:S(2)}) copy-start(bf16[160,256]{1,0:T(8,128)(2,1)} %get-tuple-element.10) | copy-start | bytes 245764
  63.4 45.2 %copy-start.11 = (bf16[160,256]{1,0:T(8,128)(2,1)S(1)}, bf16[160,256]{1,0:T(8,128)(2,1)}, u32[]{:S(2)}) copy-start(bf16[160,256]{1,0:T(8,128)(2,1)} %get-tuple-element.11) | copy-start | bytes 245764
  63.4 45.2 %copy-start.13 = (bf16[160,256]{1,0:T(8,128)(2,1)S(1)}, bf16[160,256]{1,0:T(8,128)(2,1)}, u32[]{:S(2)}) copy-start(bf16[160,256]{1,0:T(8,128)(2,1)} %copy-done.12) | copy-start | bytes 245764
  63.4 45.2 %copy-start.15 = (bf16[160,256]{1,0:T(8,128)(2,1)S(1)}, bf16[160,256]{1,0:T(8,128)(2,1)}, u32[]{:S(2)}) copy-start(bf16[160,256]{1,0:T(8,128)(2,1)} %get-tuple-element.9) | copy-start | bytes 245764
  63.4 46.9 %all-to-all-start.2 = ((bf16[16,8,1536]{2,1,0:T(8,128)(2,1)}), bf16[16,8,1536]{2,1,0:T(8,128)(2,1)S(1)}, u32[]{:S(2)}, u32[]{:S(2)}) async-start(bf16[16,8,1536]{2,1,0:T(8,128)(2,1)} %fusion.7), calls=%async_computation.2 | async-start | bytes 786432 | tf_op jit(solution)/shard_map/all_to_all | solution.py:16
  76.4 24.9 %collective-permute-start.1 = (bf16[160,1536]{1,0:T(8,128)(2,1)S(1)}, bf16[160,1536]{1,0:T(8,128)(2,1)S(1)}, u32[]{:S(2)}, u32[]{:S(2)}) collective-permute-start(bf16[160,1536]{1,0:T(8,128)(2,1)S(1)} %fusion.6), channel_id=1, source_target_pairs={{0,8},{8,16},{16,24},{24,0},{1,9},{9,17},{17,25},{25,1},{2,10},{10... | collective-permute-start | bytes 1474568 | tf_op jit(solution)/shard_map/ppermute | solution.py:30
  80.4 20.9 %collective-permute-start.2 = (bf16[160,1536]{1,0:T(8,128)(2,1)S(1)}, bf16[160,1536]{1,0:T(8,128)(2,1)S(1)}, u32[]{:S(2)}, u32[]{:S(2)}) collective-permute-start(bf16[160,1536]{1,0:T(8,128)(2,1)S(1)} %fusion.6), channel_id=1, source_target_pairs={{0,24},{8,0},{16,8},{24,16},{1,25},{9,1},{17,9},{25,17},{2,26},{10... | collective-permute-start | bytes 1474568 | tf_op jit(solution)/shard_map/ppermute | solution.py:30
  82.3 25.5 %collective-permute-start.3 = (bf16[160,1536]{1,0:T(8,128)(2,1)S(1)}, bf16[160,1536]{1,0:T(8,128)(2,1)S(1)}, u32[]{:S(2)}, u32[]{:S(2)}) collective-permute-start(bf16[160,1536]{1,0:T(8,128)(2,1)S(1)} %fusion.6), channel_id=1, source_target_pairs={{0,16},{8,24},{16,0},{24,8},{1,17},{9,25},{17,1},{25,9},{2,18},{10... | collective-permute-start | bytes 1474568 | tf_op jit(solution)/shard_map/ppermute | solution.py:30
  107.8 0.8 copy-start.19
  108.5 5.8 %copy-start.4 = (bf16[160,256]{1,0:T(8,128)(2,1)S(1)}, bf16[160,256]{1,0:T(8,128)(2,1)}, u32[]{:S(2)}) copy-start(bf16[160,256]{1,0:T(8,128)(2,1)} %copy-done.3) | copy-start | bytes 245764
  108.6 5.8 %copy-start.6 = (bf16[160,256]{1,0:T(8,128)(2,1)S(1)}, bf16[160,256]{1,0:T(8,128)(2,1)}, u32[]{:S(2)}) copy-start(bf16[160,256]{1,0:T(8,128)(2,1)} %get-tuple-element.18) | copy-start | bytes 245764
  108.6 5.8 %copy-start.8 = (bf16[160,256]{1,0:T(8,128)(2,1)S(1)}, bf16[160,256]{1,0:T(8,128)(2,1)}, u32[]{:S(2)}) copy-start(bf16[160,256]{1,0:T(8,128)(2,1)} %copy-done.7) | copy-start | bytes 245764
  108.6 5.8 %copy-start.14 = (bf16[160,256]{1,0:T(8,128)(2,1)S(1)}, bf16[160,256]{1,0:T(8,128)(2,1)}, u32[]{:S(2)}) copy-start(bf16[160,256]{1,0:T(8,128)(2,1)} %get-tuple-element.20) | copy-start | bytes 245764
  111.1 8.4 %all-to-all-start.3 = ((f32[4,1,8]{2,1,0:T(1,128)}), f32[4,1,8]{2,1,0:T(1,128)S(1)}, u32[]{:S(2)}, u32[]{:S(2)}) async-start(f32[4,1,8]{2,1,0:T(1,128)} %broadcast_in_dim.20), calls=%async_computation.3 | async-start | bytes 4096 | tf_op jit(solution)/shard_map/all_to_all | solution.py:16
where the time goes:
time: 121 us; the launch traced here: 120 us
  starting transfers between devices  60.6 us (50%)
  waiting for transfers between devices  35 us (29%)
  matrix products  16.3 us (13%)
  local copies, waits for them, and re-layouts  6.12 us (5%)
  other arithmetic  1.32 us (1%)
    all_to_all x4, starting transfers between devices, exchange(): return lax.all_to_all(x, axis, 0, 0, tiled=True)  34.4 us
    ppermute x6, waiting for transfers between devices, along_x(): return lax.ppermute(x, 'x', [(i, (i + step) % size) for i in range(size)])  27.1 us
    ppermute x6, starting transfers between devices, along_x(): return lax.ppermute(x, 'x', [(i, (i + step) % size) for i in range(size)])  22.4 us
    all_to_all x4, waiting for transfers between devices, exchange(): return lax.all_to_all(x, axis, 0, 0, tiled=True)  7.87 us
    dot_general x4, matrix products, part_for(): lax.dot_general(up, w_up[0], unit_contract, preferred_element_type=jnp.fl...  5.3 us
    ppermute x2, starting transfers between devices, swap_cores(): return lax.ppermute(x, 'core', [(0, 1), (1, 0)])  3.83 us
    dot_general x1, matrix products, on_device(): lax.dot_general(gathered, in_order(grad_gate[0]), first, preferred_elemen...  2.74 us
    dot_general x2, matrix products, rows_from(): lax.dot_general(chosen, line_normed, first, preferred_element_type=jnp.fl...  2.62 us
  transfers between devices with their start and end apart: 12, of which 7 were waited for; matrix products, arithmetic and copies ran while one was open for 14% of the time, Pallas kernels for 0%

commit v1 on v0

--- a/solution.py
+++ b/solution.py
@@ -112,11 +112,15 @@
             ]
         )
 
+    gate_rows, up_rows = lax.optimization_barrier(
+        (in_order(grad_gate[0]), in_order(grad_up[0]))
+    )
+    gathered = lax.optimization_barrier(gathered)
     new_gate = lax.dot_general(
-        gathered, in_order(grad_gate[0]), first, preferred_element_type=jnp.float32
+        gathered, gate_rows, first, preferred_element_type=jnp.float32
     )
     new_up = lax.dot_general(
-        gathered, in_order(grad_up[0]), first, preferred_element_type=jnp.float32
+        gathered, up_rows, first, preferred_element_type=jnp.float32
     )
 
     line_sum = (part_for(0) + arriving[0] + arriving[1] + arriving[2]).astype(jnp.bfloat16)

time: 121 us -> 123 us (1.017)
  the two profiles are of different devices: /device:TPU:2 before, /device:TPU:32 now
where the time goes in v1:
time: 123 us; the launch traced here: 122 us
  starting transfers between devices  59.7 us (49%)
  waiting for transfers between devices  37.2 us (30%)
  matrix products  16.4 us (13%)
  local copies, waits for them, and re-layouts  4.45 us (4%)
  other arithmetic  3.07 us (2%)
    all_to_all x4, starting transfers between devices, exchange(): return lax.all_to_all(x, axis, 0, 0, tiled=True)  36.2 us
    ppermute x6, waiting for transfers between devices, along_x(): return lax.ppermute(x, 'x', [(i, (i + step) % size) for i in range(size)])  34.6 us
    ppermute x6, starting transfers between devices, along_x(): return lax.ppermute(x, 'x', [(i, (i + step) % size) for i in range(size)])  19.2 us
    dot_general x4, matrix products, part_for(): lax.dot_general(up, w_up[0], unit_contract, preferred_element_type=jnp.fl...  4.51 us
    ppermute x2, starting transfers between devices, swap_cores(): return lax.ppermute(x, 'core', [(0, 1), (1, 0)])  4.32 us
    dot_general x1, matrix products, on_device(): lax.dot_general(gathered, up_rows, first, preferred_element_type=jnp.floa...  2.68 us
    dot_general x2, matrix products, rows_from(): lax.dot_general(chosen, line_normed, first, preferred_element_type=jnp.fl...  2.62 us
    all_to_all x4, waiting for transfers between devices, exchange(): return lax.all_to_all(x, axis, 0, 0, tiled=True)  2.54 us
  transfers between devices with their start and end apart: 12, of which 5 were waited for; matrix products, arithmetic and copies ran while one was open for 17% of the time, Pallas kernels for 0%

profile of v1, /device:TPU:32, one launch (start us, length us, event | category | flops | bytes accessed | tf_op | source)
XLA Modules:
  0.0 121.9 jit_solution(2647066586519712735)
XLA Ops:
  0.6 0.0 copy-start
  0.7 1.0 fusion.62
  1.6 0.6 broadcast_in_dim.15
  2.2 4.5 %all-to-all-start = ((f32[4,1,8]{2,1,0:T(1,128)}), f32[4,1,8]{2,1,0:T(1,128)S(1)}, u32[]{:S(2)}, u32[]{:S(2)}) async-start(f32[4,1,8]{2,1,0:T(1,128)} %broadcast_in_dim.15), calls=%async_computation | async-start | bytes 4096 | tf_op jit(solution)/shard_map/all_to_all | solution.py:16
  6.7 1.9 %dynamic-slice_bitcast_fusion.3 = (bf16[160,256]{1,0:T(8,128)(2,1)}, bf16[160,256]{1,0:T(8,128)(2,1)S(1)}, bf16[160,256]{1,0:T(8,128)(2,1)S(1)}, bf16[160,256]{1...) fusion(bf16[1,640,256]{2,1,0:T(8,128)(2,1)} %param.15, ...), kind=kLoop, calls=%fused_computation.58 | loop fusion | bytes 1310736 | tf_op jit(solution)/shard_map/dynamic_slice | solution.py:108
  8.6 0.4 fusion.14
  9.1 1.2 fusion.4
  10.2 4.7 %collective-permute-start.6 = (bf16[160,1536]{1,0:T(8,128)(2,1)}, bf16[160,1536]{1,0:T(8,128)(2,1)}, u32[]{:S(2)}, u32[]{:S(2)}) collective-permute-start(bf16[160,1536]{1,0:T(8,128)(2,1)} %fusion.4), channel_id=1, source_target_pairs={{0,24},{8,0},{16,8},{24,16},{1,25},{9,1},{17,9},{25,17},{2,26},{10... | collective-permute-start | bytes 1474568 | tf_op jit(solution)/shard_map/ppermute | solution.py:30
  14.9 0.1 copy.21
  15.0 0.1 copy.22
  15.1 0.4 fusion.16
  15.6 0.1 fusion.57
  15.7 0.8 broadcast_in_dim.16
  16.5 15.2 %all-to-all-start.1 = ((bf16[16,8,1664]{2,1,0:T(8,128)(2,1)}), bf16[16,8,1664]{2,1,0:T(8,128)(2,1)S(1)}, u32[]{:S(2)}, u32[]{:S(2)}) async-start(bf16[16,8,1664]{2,1,0:T(8,128)(2,1)} %broadcast_in_dim.16), calls=%async_computation.1 | async-start | bytes 851968 | tf_op jit(solution)/shard_map/all_to_all | solution.py:16
  31.7 1.2 fusion.3
  32.9 1.9 %collective-permute-start.5 = (bf16[160,1536]{1,0:T(8,128)(2,1)}, bf16[160,1536]{1,0:T(8,128)(2,1)S(1)}, u32[]{:S(2)}, u32[]{:S(2)}) collective-permute-start(bf16[160,1536]{1,0:T(8,128)(2,1)} %fusion.3), channel_id=1, source_target_pairs={{0,8},{8,16},{16,24},{24,0},{1,9},{9,17},{17,25},{25,1},{2,10},{10... | collective-permute-start | bytes 1474568 | tf_op jit(solution)/shard_map/ppermute | solution.py:30
  34.8 0.4 fusion.18
  35.2 0.4 fusion.2
  35.6 4.2 %collective-permute-start.4 = (bf16[160,1536]{1,0:T(8,128)(2,1)S(1)}, bf16[160,1536]{1,0:T(8,128)(2,1)}, u32[]{:S(2)}, u32[]{:S(2)}) collective-permute-start(bf16[160,1536]{1,0:T(8,128)(2,1)S(1)} %fusion.2), channel_id=1, source_target_pairs={{0,16},{8,24},{16,0},{24,8},{1,17},{9,25},{17,1},{25,9},{2,18},{10... | collective-permute-start | bytes 1474568 | tf_op jit(solution)/shard_map/ppermute | solution.py:30
  39.9 1.3 %fusion.20 = f32[160,1536]{1,0:T(8,128)S(1)} fusion(bf16[1,1536,256]{2,1,0:T(8,128)(2,1)S(1)} %copy-done, bf16[1,640,256]{2,1,0:T(8,128)(2,1)} %param.14, s32[]{:T(128)S(6)} %select_n.69), kind=kOutput, calls=%fused_computation.29 | convolution fusion | flops 125829120 | bytes 1851396 | tf_op jit(solution)/shard_map/dot_general | solution.py:54
  41.2 17.4 %collective-permute-done.5 = bf16[160,1536]{1,0:T(8,128)(2,1)S(1)} collective-permute-done((bf16[160,1536]{1,0:T(8,128)(2,1)}, bf16[160,1536]{1,0:T(8,128)(2,1)S(1)}, u32[]{:S(2)}, u32[]{:S(2)}) %collective-permute-start.5) | collective-permute-done | bytes 491552 | tf_op jit(solution)/shard_map/ppermute | solution.py:30
  58.6 1.7 %add_convert_fusion = bf16[160,1536]{1,0:T(8,128)(2,1)S(1)} fusion(bf16[160,1536]{1,0:T(8,128)(2,1)} %collective-permute-done.6, bf16[160,1536]{1,0:T(8,128)(2,1)S(1)} %collective-permute-done.5, bf16[160,1536]{1,0:T(8,128)(2,1)} %collective-permute-done.4, f32[160,1536]{1,0:T(8,128)S(1)} %fusion.20, bf16[1,1536,256]{2,1,0:T(8,128)(2,1)S(1)} %copy-done.1, ...), kind=kOutput, calls=%fused_computation.18 | convolution fusion | flops 127795200 | bytes 3817476 | tf_op jit(solution)/shard_map/dot_general | solution.py:56
  60.3 1.9 %collective-permute-start.7 = (bf16[160,1536]{1,0:T(8,128)(2,1)S(1)}, bf16[160,1536]{1,0:T(8,128)(2,1)}, u32[]{:S(2)}, u32[]{:S(2)}) collective-permute-start(bf16[160,1536]{1,0:T(8,128)(2,1)S(1)} %add_convert_fusion), channel_id=1, source_target_pairs={{0,128},{128,0},{1,129},{129,1},{2,130},{130,2},{3,131},{131,3},{4... | collective-permute-start | bytes 1474568 | tf_op jit(solution)/shard_map/ppermute | solution.py:34
  62.2 0.1 fusion.42
  62.3 0.2 slice_reduce_fusion.1
  62.5 1.2 convolution_convert_fusion.2
  63.7 2.4 %collective-permute-start = (bf16[160,1536]{1,0:T(8,128)(2,1)}, bf16[160,1536]{1,0:T(8,128)(2,1)}, u32[]{:S(2)}, u32[]{:S(2)}) collective-permute-start(bf16[160,1536]{1,0:T(8,128)(2,1)} %convolution_convert_fusion.2), channel_id=1, source_target_pairs={{0,128},{128,0},{1,129},{129,1},{2,130},{130,2},{3,131},{131,3},{4... | collective-permute-start | bytes 1474568 | tf_op jit(solution)/shard_map/ppermute | solution.py:34
  66.1 1.3 %fusion.26 = f32[128,1536]{1,0:T(8,128)S(1)} fusion(bf16[160,1536]{1,0:T(8,128)(2,1)} %collective-permute-done.7, s32[128]{0:T(128)S(1)} %get-tuple-element.10, s32[128]{0:T(128)S(1)} %get-tuple-element.9), kind=kOutput, calls=%fused_computation.42 | convolution fusion | flops 62976000 | bytes 1278976 | tf_op jit(solution)/shard_map/dot_general | solution.py:128
  67.5 0.2 slice_reduce_fusion.3
  67.7 1.1 fusion.7
  68.8 12.0 %all-to-all-start.2 = ((bf16[16,8,1536]{2,1,0:T(8,128)(2,1)}), bf16[16,8,1536]{2,1,0:T(8,128)(2,1)S(1)}, u32[]{:S(2)}, u32[]{:S(2)}) async-start(bf16[16,8,1536]{2,1,0:T(8,128)(2,1)} %fusion.7), calls=%async_computation.2 | async-start | bytes 786432 | tf_op jit(solution)/shard_map/all_to_all | solution.py:16
  80.8 1.4 %fusion.6 = bf16[160,1536]{1,0:T(8,128)(2,1)S(1)} fusion(bf16[160,1536]{1,0:T(8,128)(2,1)} %collective-permute-done, bf16[128,1664]{1,0:T(8,128)(2,1)S(1)} %bitcast.65, s32[128]{0:T(128)S(1)} %get-tuple-element.8, s32[128]{0:T(128)S(1)} %get-tuple-element.7), kind=kOutput, calls=%fused_computation.15 | convolution fusion | flops 63467520 | bytes 1377280 | tf_op jit(solution)/shard_map/dot_general | solution.py:95
  82.2 2.6 %collective-permute-start.3 = (bf16[160,1536]{1,0:T(8,128)(2,1)S(1)}, bf16[160,1536]{1,0:T(8,128)(2,1)S(1)}, u32[]{:S(2)}, u32[]{:S(2)}) collective-permute-start(bf16[160,1536]{1,0:T(8,128)(2,1)S(1)} %fusion.6), channel_id=1, source_target_pairs={{0,16},{8,24},{16,0},{24,8},{1,17},{9,25},{17,1},{25,9},{2,18},{10... | collective-permute-start | bytes 1474568 | tf_op jit(solution)/shard_map/ppermute | solution.py:30
  84.8 1.9 %collective-permute-start.2 = (bf16[160,1536]{1,0:T(8,128)(2,1)S(1)}, bf16[160,1536]{1,0:T(8,128)(2,1)S(1)}, u32[]{:S(2)}, u32[]{:S(2)}) collective-permute-start(bf16[160,1536]{1,0:T(8,128)(2,1)S(1)} %fusion.6), channel_id=1, source_target_pairs={{0,24},{8,0},{16,8},{24,16},{1,25},{9,1},{17,9},{25,17},{2,26},{10... | collective-permute-start | bytes 1474568 | tf_op jit(solution)/shard_map/ppermute | solution.py:30
  86.8 3.9 %collective-permute-start.1 = (bf16[160,1536]{1,0:T(8,128)(2,1)S(1)}, bf16[160,1536]{1,0:T(8,128)(2,1)S(1)}, u32[]{:S(2)}, u32[]{:S(2)}) collective-permute-start(bf16[160,1536]{1,0:T(8,128)(2,1)S(1)} %fusion.6), channel_id=1, source_target_pairs={{0,8},{8,16},{16,24},{24,0},{1,9},{9,17},{17,25},{25,1},{2,10},{10... | collective-permute-start | bytes 1474568 | tf_op jit(solution)/shard_map/ppermute | solution.py:30
  90.7 0.7 pad_maximum_fusion.2
  91.5 8.3 %collective-permute-done.3 = bf16[160,1536]{1,0:T(8,128)(2,1)S(1)} collective-permute-done((bf16[160,1536]{1,0:T(8,128)(2,1)S(1)}, bf16[160,1536]{1,0:T(8,128)(2,1)S(1)}, u32[]{:S(2)}, u32[]{:S(2)}) %collective-permute-start.3) | collective-permute-done | bytes 491552 | tf_op jit(solution)/shard_map/ppermute | solution.py:30
  99.8 6.0 %collective-permute-done.2 = bf16[160,1536]{1,0:T(8,128)(2,1)S(1)} collective-permute-done((bf16[160,1536]{1,0:T(8,128)(2,1)S(1)}, bf16[160,1536]{1,0:T(8,128)(2,1)S(1)}, u32[]{:S(2)}, u32[]{:S(2)}) %collective-permute-start.2) | collective-permute-done | bytes 491552 | tf_op jit(solution)/shard_map/ppermute | solution.py:30
  105.8 2.9 %collective-permute-done.1 = bf16[160,1536]{1,0:T(8,128)(2,1)S(1)} collective-permute-done((bf16[160,1536]{1,0:T(8,128)(2,1)S(1)}, bf16[160,1536]{1,0:T(8,128)(2,1)S(1)}, u32[]{:S(2)}, u32[]{:S(2)}) %collective-permute-start.1) | collective-permute-done | bytes 491552 | tf_op jit(solution)/shard_map/ppermute | solution.py:30
  108.7 0.1 pad_maximum_fusion
  108.9 1.7 %fusion = bf16[1,1536,256]{2,1,0:T(8,128)(2,1)} fusion(bf16[640,1536]{1,0:T(8,128)(2,1)S(1)} %pad_maximum_fusion, bf16[640,256]{1,0:T(8,128)(2,1)S(1)} %pad_maximum_fusion.1), kind=kOutput, calls=%fused_computation.7 | convolution fusion | flops 503709696 | bytes 3080192 | tf_op jit(solution)/shard_map/dot_general | solution.py:119
  110.6 0.1 convert_reduce_fusion
  110.7 0.2 fusion.58
  110.9 0.6 broadcast_in_dim.20
  111.5 4.5 %all-to-all-start.3 = ((f32[4,1,8]{2,1,0:T(1,128)}), f32[4,1,8]{2,1,0:T(1,128)S(1)}, u32[]{:S(2)}, u32[]{:S(2)}) async-start(f32[4,1,8]{2,1,0:T(1,128)} %broadcast_in_dim.20), calls=%async_computation.3 | async-start | bytes 4096 | tf_op jit(solution)/shard_map/all_to_all | solution.py:16
  116.0 2.7 %fusion.1 = bf16[1,1536,256]{2,1,0:T(8,128)(2,1)} fusion(bf16[640,1536]{1,0:T(8,128)(2,1)S(1)} %pad_maximum_fusion, bf16[640,256]{1,0:T(8,128)(2,1)} %pad_maximum_fusion.2), kind=kOutput, calls=%fused_computation.8 | convolution fusion | flops 503709696 | bytes 3080192 | tf_op jit(solution)/shard_map/dot_general | solution.py:122
  118.7 2.5 %all-to-all-done.3 = f32[4,1,8]{2,1,0:T(1,128)S(1)} async-done(((f32[4,1,8]{2,1,0:T(1,128)}), f32[4,1,8]{2,1,0:T(1,128)S(1)}, u32[]{:S(2)}, u32[]{:S(2)}) %all-to-all-start.3) | async-done | bytes 160 | tf_op jit(solution)/shard_map/all_to_all | solution.py:16
  121.2 0.7 fusion.61
  (52 shorter events, 0.2 us)
Async XLA Ops:
  0.6 8.0 %copy-start = (bf16[1,1536,256]{2,1,0:T(8,128)(2,1)S(1)}, bf16[1,1536,256]{2,1,0:T(8,128)(2,1)}, u32[]{:S(2)}) copy-start(bf16[1,1536,256]{2,1,0:T(8,128)(2,1)} %param.12) | copy-start | bytes 2359300
  0.6 8.4 %copy-start.1 = (bf16[1,1536,256]{2,1,0:T(8,128)(2,1)S(1)}, bf16[1,1536,256]{2,1,0:T(8,128)(2,1)}, u32[]{:S(2)}) copy-start(bf16[1,1536,256]{2,1,0:T(8,128)(2,1)} %param.13) | copy-start | bytes 2359300
  2.2 13.3 %all-to-all-start = ((f32[4,1,8]{2,1,0:T(1,128)}), f32[4,1,8]{2,1,0:T(1,128)S(1)}, u32[]{:S(2)}, u32[]{:S(2)}) async-start(f32[4,1,8]{2,1,0:T(1,128)} %broadcast_in_dim.15), calls=%async_computation | async-start | bytes 4096 | tf_op jit(solution)/shard_map/all_to_all | solution.py:16
  8.6 1.7 %copy-start.6 = (bf16[160,256]{1,0:T(8,128)(2,1)}, bf16[160,256]{1,0:T(8,128)(2,1)S(1)}, u32[]{:S(2)}) copy-start(bf16[160,256]{1,0:T(8,128)(2,1)S(1)} %get-tuple-element.15) | copy-start | bytes 245764
  8.6 6.5 %copy-start.2 = (bf16[160,256]{1,0:T(8,128)(2,1)}, bf16[160,256]{1,0:T(8,128)(2,1)S(1)}, u32[]{:S(2)}) copy-start(bf16[160,256]{1,0:T(8,128)(2,1)S(1)} %get-tuple-element.23) | copy-start | bytes 245764
  8.6 23.1 %copy-start.4 = (bf16[160,256]{1,0:T(8,128)(2,1)}, bf16[160,256]{1,0:T(8,128)(2,1)S(1)}, u32[]{:S(2)}) copy-start(bf16[160,256]{1,0:T(8,128)(2,1)S(1)} %get-tuple-element.14) | copy-start | bytes 245764
  8.6 26.6 %copy-start.8 = (bf16[160,256]{1,0:T(8,128)(2,1)}, bf16[160,256]{1,0:T(8,128)(2,1)S(1)}, u32[]{:S(2)}) copy-start(bf16[160,256]{1,0:T(8,128)(2,1)S(1)} %get-tuple-element.16) | copy-start | bytes 245764
  8.6 6.3 %copy-start.17 = (s32[8,2]{0,1:T(2,128)S(1)}, s32[8,2]{0,1:T(2,128)}, u32[]{:S(2)}) copy-start(s32[8,2]{0,1:T(2,128)} %param.10) | copy-start | bytes 196
  8.6 6.4 %copy-start.18 = (s32[8,2]{0,1:T(2,128)S(1)}, s32[8,2]{0,1:T(2,128)}, u32[]{:S(2)}) copy-start(s32[8,2]{0,1:T(2,128)} %param.11) | copy-start | bytes 196
  9.0 6.5 %copy-start.10 = (bf16[8,1536]{1,0:T(8,128)(2,1)S(1)}, bf16[8,1536]{1,0:T(8,128)(2,1)}, u32[]{:S(2)}) copy-start(bf16[8,1536]{1,0:T(8,128)(2,1)} %param.8) | copy-start | bytes 73732
  9.0 6.5 %copy-start.14 = (f32[1536]{0:T(1024)S(1)}, f32[1536]{0:T(1024)}, u32[]{:S(2)}) copy-start(f32[1536]{0:T(1024)} %param.9) | copy-start | bytes 18436
  10.2 30.9 %collective-permute-start.6 = (bf16[160,1536]{1,0:T(8,128)(2,1)}, bf16[160,1536]{1,0:T(8,128)(2,1)}, u32[]{:S(2)}, u32[]{:S(2)}) collective-permute-start(bf16[160,1536]{1,0:T(8,128)(2,1)} %fusion.4), channel_id=1, source_target_pairs={{0,24},{8,0},{16,8},{24,16},{1,25},{9,1},{17,9},{25,17},{2,26},{10... | collective-permute-start | bytes 1474568 | tf_op jit(solution)/shard_map/ppermute | solution.py:30
  15.6 19.6 %copy-start.15 = (f32[8]{0:T(128)}, f32[8]{0:T(128)S(1)}, u32[]{:S(2)}) copy-start(f32[8]{0:T(128)S(1)} %add_rsqrt_fusion) | copy-start | bytes 100
  16.5 45.7 %all-to-all-start.1 = ((bf16[16,8,1664]{2,1,0:T(8,128)(2,1)}), bf16[16,8,1664]{2,1,0:T(8,128)(2,1)S(1)}, u32[]{:S(2)}, u32[]{:S(2)}) async-start(bf16[16,8,1664]{2,1,0:T(8,128)(2,1)} %broadcast_in_dim.16), calls=%async_computation.1 | async-start | bytes 851968 | tf_op jit(solution)/shard_map/all_to_all | solution.py:16
  32.9 25.7 %collective-permute-start.5 = (bf16[160,1536]{1,0:T(8,128)(2,1)}, bf16[160,1536]{1,0:T(8,128)(2,1)S(1)}, u32[]{:S(2)}, u32[]{:S(2)}) collective-permute-start(bf16[160,1536]{1,0:T(8,128)(2,1)} %fusion.3), channel_id=1, source_target_pairs={{0,8},{8,16},{16,24},{24,0},{1,9},{9,17},{17,25},{25,1},{2,10},{10... | collective-permute-start | bytes 1474568 | tf_op jit(solution)/shard_map/ppermute | solution.py:30
  35.6 22.9 %collective-permute-start.4 = (bf16[160,1536]{1,0:T(8,128)(2,1)S(1)}, bf16[160,1536]{1,0:T(8,128)(2,1)}, u32[]{:S(2)}, u32[]{:S(2)}) collective-permute-start(bf16[160,1536]{1,0:T(8,128)(2,1)S(1)} %fusion.2), channel_id=1, source_target_pairs={{0,16},{8,24},{16,0},{24,8},{1,17},{9,25},{17,1},{25,9},{2,18},{10... | collective-permute-start | bytes 1474568 | tf_op jit(solution)/shard_map/ppermute | solution.py:30
  60.3 5.8 %collective-permute-start.7 = (bf16[160,1536]{1,0:T(8,128)(2,1)S(1)}, bf16[160,1536]{1,0:T(8,128)(2,1)}, u32[]{:S(2)}, u32[]{:S(2)}) collective-permute-start(bf16[160,1536]{1,0:T(8,128)(2,1)S(1)} %add_convert_fusion), channel_id=1, source_target_pairs={{0,128},{128,0},{1,129},{129,1},{2,130},{130,2},{3,131},{131,3},{4... | collective-permute-start | bytes 1474568 | tf_op jit(solution)/shard_map/ppermute | solution.py:34
  63.7 17.1 %collective-permute-start = (bf16[160,1536]{1,0:T(8,128)(2,1)}, bf16[160,1536]{1,0:T(8,128)(2,1)}, u32[]{:S(2)}, u32[]{:S(2)}) collective-permute-start(bf16[160,1536]{1,0:T(8,128)(2,1)} %convolution_convert_fusion.2), channel_id=1, source_target_pairs={{0,128},{128,0},{1,129},{129,1},{2,130},{130,2},{3,131},{131,3},{4... | collective-permute-start | bytes 1474568 | tf_op jit(solution)/shard_map/ppermute | solution.py:34
  67.5 23.2 %copy-start.5 = (bf16[160,256]{1,0:T(8,128)(2,1)S(1)}, bf16[160,256]{1,0:T(8,128)(2,1)}, u32[]{:S(2)}) copy-start(bf16[160,256]{1,0:T(8,128)(2,1)} %copy-done.4) | copy-start | bytes 245764
  67.5 23.2 %copy-start.7 = (bf16[160,256]{1,0:T(8,128)(2,1)S(1)}, bf16[160,256]{1,0:T(8,128)(2,1)}, u32[]{:S(2)}) copy-start(bf16[160,256]{1,0:T(8,128)(2,1)} %copy-done.6) | copy-start | bytes 245764
  67.5 23.2 %copy-start.9 = (bf16[160,256]{1,0:T(8,128)(2,1)S(1)}, bf16[160,256]{1,0:T(8,128)(2,1)}, u32[]{:S(2)}) copy-start(bf16[160,256]{1,0:T(8,128)(2,1)} %copy-done.8) | copy-start | bytes 245764
  67.5 23.2 %copy-start.13 = (bf16[160,256]{1,0:T(8,128)(2,1)S(1)}, bf16[160,256]{1,0:T(8,128)(2,1)}, u32[]{:S(2)}) copy-start(bf16[160,256]{1,0:T(8,128)(2,1)} %get-tuple-element.13) | copy-start | bytes 245764
  67.7 23.8 %copy-start.3 = (bf16[160,256]{1,0:T(8,128)(2,1)S(1)}, bf16[160,256]{1,0:T(8,128)(2,1)}, u32[]{:S(2)}) copy-start(bf16[160,256]{1,0:T(8,128)(2,1)} %copy-done.2) | copy-start | bytes 245764
  67.7 23.8 %copy-start.12 = (bf16[160,256]{1,0:T(8,128)(2,1)S(1)}, bf16[160,256]{1,0:T(8,128)(2,1)}, u32[]{:S(2)}) copy-start(bf16[160,256]{1,0:T(8,128)(2,1)} %get-tuple-element.24) | copy-start | bytes 245764
  68.8 41.8 %all-to-all-start.2 = ((bf16[16,8,1536]{2,1,0:T(8,128)(2,1)}), bf16[16,8,1536]{2,1,0:T(8,128)(2,1)S(1)}, u32[]{:S(2)}, u32[]{:S(2)}) async-start(bf16[16,8,1536]{2,1,0:T(8,128)(2,1)} %fusion.7), calls=%async_computation.2 | async-start | bytes 786432 | tf_op jit(solution)/shard_map/all_to_all | solution.py:16
  82.2 17.5 %collective-permute-start.3 = (bf16[160,1536]{1,0:T(8,128)(2,1)S(1)}, bf16[160,1536]{1,0:T(8,128)(2,1)S(1)}, u32[]{:S(2)}, u32[]{:S(2)}) collective-permute-start(bf16[160,1536]{1,0:T(8,128)(2,1)S(1)} %fusion.6), channel_id=1, source_target_pairs={{0,16},{8,24},{16,0},{24,8},{1,17},{9,25},{17,1},{25,9},{2,18},{10... | collective-permute-start | bytes 1474568 | tf_op jit(solution)/shard_map/ppermute | solution.py:30
  84.8 21.0 %collective-permute-start.2 = (bf16[160,1536]{1,0:T(8,128)(2,1)S(1)}, bf16[160,1536]{1,0:T(8,128)(2,1)S(1)}, u32[]{:S(2)}, u32[]{:S(2)}) collective-permute-start(bf16[160,1536]{1,0:T(8,128)(2,1)S(1)} %fusion.6), channel_id=1, source_target_pairs={{0,24},{8,0},{16,8},{24,16},{1,25},{9,1},{17,9},{25,17},{2,26},{10... | collective-permute-start | bytes 1474568 | tf_op jit(solution)/shard_map/ppermute | solution.py:30
  86.8 22.0 %collective-permute-start.1 = (bf16[160,1536]{1,0:T(8,128)(2,1)S(1)}, bf16[160,1536]{1,0:T(8,128)(2,1)S(1)}, u32[]{:S(2)}, u32[]{:S(2)}) collective-permute-start(bf16[160,1536]{1,0:T(8,128)(2,1)S(1)} %fusion.6), channel_id=1, source_target_pairs={{0,8},{8,16},{16,24},{24,0},{1,9},{9,17},{17,25},{25,1},{2,10},{10... | collective-permute-start | bytes 1474568 | tf_op jit(solution)/shard_map/ppermute | solution.py:30
  108.9 1.8 %copy-start.11 = (bf16[8,1536]{1,0:T(8,128)(2,1)S(1)}, bf16[8,1536]{1,0:T(8,128)(2,1)}, u32[]{:S(2)}) copy-start(bf16[8,1536]{1,0:T(8,128)(2,1)} %param.8) | copy-start | bytes 73732
  108.9 1.8 %copy-start.16 = (f32[8]{0:T(128)S(1)}, f32[8]{0:T(128)}, u32[]{:S(2)}) copy-start(f32[8]{0:T(128)} %copy-done.15) | copy-start | bytes 100
  111.5 9.7 %all-to-all-start.3 = ((f32[4,1,8]{2,1,0:T(1,128)}), f32[4,1,8]{2,1,0:T(1,128)S(1)}, u32[]{:S(2)}, u32[]{:S(2)}) async-start(f32[4,1,8]{2,1,0:T(1,128)} %broadcast_in_dim.20), calls=%async_computation.3 | async-start | bytes 4096 | tf_op jit(solution)/shard_map/all_to_all | solution.py:16

commit v2 on v1

--- a/solution.py
+++ b/solution.py
@@ -100,7 +100,10 @@
     from_partner = swap_cores(for_partner)
     own_rows = rows_from(to_mine) + from_partner
     steps = (0, 1, 3, 2)
-    gathered = jnp.concatenate([own_rows] + [along_x(own_rows, step) for step in steps[1:]])
+    pieces = [own_rows]
+    for step in steps[1:]:
+        pieces.append(along_x(own_rows, step))
+    gathered = jnp.concatenate(pieces)
 
     def in_order(cotangent):
         return jnp.concatenate(

time: 123 us -> 123 us (level)
  no operation moved by 1% of the time
where the time goes in v2:
time: 123 us; the launch traced here: 122 us
  starting transfers between devices  59.7 us (49%)
  waiting for transfers between devices  37.2 us (30%)
  matrix products  16.4 us (13%)
  local copies, waits for them, and re-layouts  4.45 us (4%)
  other arithmetic  3.07 us (2%)
    all_to_all x4, starting transfers between devices, exchange(): return lax.all_to_all(x, axis, 0, 0, tiled=True)  36.2 us
    ppermute x6, waiting for transfers between devices, along_x(): return lax.ppermute(x, 'x', [(i, (i + step) % size) for i in range(size)])  34.6 us
    ppermute x6, starting transfers between devices, along_x(): return lax.ppermute(x, 'x', [(i, (i + step) % size) for i in range(size)])  19.2 us
    dot_general x4, matrix products, part_for(): lax.dot_general(up, w_up[0], unit_contract, preferred_element_type=jnp.fl...  4.51 us
    ppermute x2, starting transfers between devices, swap_cores(): return lax.ppermute(x, 'core', [(0, 1), (1, 0)])  4.32 us
    dot_general x1, matrix products, on_device(): lax.dot_general(gathered, up_rows, first, preferred_element_type=jnp.floa...  2.68 us
    dot_general x2, matrix products, rows_from(): lax.dot_general(chosen, line_normed, first, preferred_element_type=jnp.fl...  2.62 us
    all_to_all x4, waiting for transfers between devices, exchange(): return lax.all_to_all(x, axis, 0, 0, tiled=True)  2.54 us
  transfers between devices with their start and end apart: 12, of which 5 were waited for; matrix products, arithmetic and copies ran while one was open for 17% of the time, Pallas kernels for 0%

profile of v2, /device:TPU:32, one launch (start us, length us, event | category | flops | bytes accessed | tf_op | source)
XLA Modules:
  0.0 121.9 jit_solution(2647066586519712735)
XLA Ops:
  0.6 0.0 copy-start
  0.7 1.0 fusion.62
  1.6 0.6 broadcast_in_dim.15
  2.2 4.5 %all-to-all-start = ((f32[4,1,8]{2,1,0:T(1,128)}), f32[4,1,8]{2,1,0:T(1,128)S(1)}, u32[]{:S(2)}, u32[]{:S(2)}) async-start(f32[4,1,8]{2,1,0:T(1,128)} %broadcast_in_dim.15), calls=%async_computation | async-start | bytes 4096 | tf_op jit(solution)/shard_map/all_to_all | solution.py:16
  6.7 1.9 %dynamic-slice_bitcast_fusion.3 = (bf16[160,256]{1,0:T(8,128)(2,1)}, bf16[160,256]{1,0:T(8,128)(2,1)S(1)}, bf16[160,256]{1,0:T(8,128)(2,1)S(1)}, bf16[160,256]{1...) fusion(bf16[1,640,256]{2,1,0:T(8,128)(2,1)} %param.15, ...), kind=kLoop, calls=%fused_computation.58 | loop fusion | bytes 1310736 | tf_op jit(solution)/shard_map/dynamic_slice | solution.py:111
  8.6 0.4 fusion.14
  9.1 1.2 fusion.4
  10.2 4.7 %collective-permute-start.6 = (bf16[160,1536]{1,0:T(8,128)(2,1)}, bf16[160,1536]{1,0:T(8,128)(2,1)}, u32[]{:S(2)}, u32[]{:S(2)}) collective-permute-start(bf16[160,1536]{1,0:T(8,128)(2,1)} %fusion.4), channel_id=1, source_target_pairs={{0,24},{8,0},{16,8},{24,16},{1,25},{9,1},{17,9},{25,17},{2,26},{10... | collective-permute-start | bytes 1474568 | tf_op jit(solution)/shard_map/ppermute | solution.py:30
  14.9 0.1 copy.21
  15.0 0.1 copy.22
  15.1 0.4 fusion.16
  15.6 0.1 fusion.57
  15.7 0.8 broadcast_in_dim.16
  16.5 15.2 %all-to-all-start.1 = ((bf16[16,8,1664]{2,1,0:T(8,128)(2,1)}), bf16[16,8,1664]{2,1,0:T(8,128)(2,1)S(1)}, u32[]{:S(2)}, u32[]{:S(2)}) async-start(bf16[16,8,1664]{2,1,0:T(8,128)(2,1)} %broadcast_in_dim.16), calls=%async_computation.1 | async-start | bytes 851968 | tf_op jit(solution)/shard_map/all_to_all | solution.py:16
  31.7 1.2 fusion.3
  32.9 1.9 %collective-permute-start.5 = (bf16[160,1536]{1,0:T(8,128)(2,1)}, bf16[160,1536]{1,0:T(8,128)(2,1)S(1)}, u32[]{:S(2)}, u32[]{:S(2)}) collective-permute-start(bf16[160,1536]{1,0:T(8,128)(2,1)} %fusion.3), channel_id=1, source_target_pairs={{0,8},{8,16},{16,24},{24,0},{1,9},{9,17},{17,25},{25,1},{2,10},{10... | collective-permute-start | bytes 1474568 | tf_op jit(solution)/shard_map/ppermute | solution.py:30
  34.8 0.4 fusion.18
  35.2 0.4 fusion.2
  35.6 4.2 %collective-permute-start.4 = (bf16[160,1536]{1,0:T(8,128)(2,1)S(1)}, bf16[160,1536]{1,0:T(8,128)(2,1)}, u32[]{:S(2)}, u32[]{:S(2)}) collective-permute-start(bf16[160,1536]{1,0:T(8,128)(2,1)S(1)} %fusion.2), channel_id=1, source_target_pairs={{0,16},{8,24},{16,0},{24,8},{1,17},{9,25},{17,1},{25,9},{2,18},{10... | collective-permute-start | bytes 1474568 | tf_op jit(solution)/shard_map/ppermute | solution.py:30
  39.9 1.3 %fusion.20 = f32[160,1536]{1,0:T(8,128)S(1)} fusion(bf16[1,1536,256]{2,1,0:T(8,128)(2,1)S(1)} %copy-done, bf16[1,640,256]{2,1,0:T(8,128)(2,1)} %param.14, s32[]{:T(128)S(6)} %select_n.69), kind=kOutput, calls=%fused_computation.29 | convolution fusion | flops 125829120 | bytes 1851396 | tf_op jit(solution)/shard_map/dot_general | solution.py:54
  41.2 17.4 %collective-permute-done.5 = bf16[160,1536]{1,0:T(8,128)(2,1)S(1)} collective-permute-done((bf16[160,1536]{1,0:T(8,128)(2,1)}, bf16[160,1536]{1,0:T(8,128)(2,1)S(1)}, u32[]{:S(2)}, u32[]{:S(2)}) %collective-permute-start.5) | collective-permute-done | bytes 491552 | tf_op jit(solution)/shard_map/ppermute | solution.py:30
  58.6 1.7 %add_convert_fusion = bf16[160,1536]{1,0:T(8,128)(2,1)S(1)} fusion(bf16[160,1536]{1,0:T(8,128)(2,1)} %collective-permute-done.6, bf16[160,1536]{1,0:T(8,128)(2,1)S(1)} %collective-permute-done.5, bf16[160,1536]{1,0:T(8,128)(2,1)} %collective-permute-done.4, f32[160,1536]{1,0:T(8,128)S(1)} %fusion.20, bf16[1,1536,256]{2,1,0:T(8,128)(2,1)S(1)} %copy-done.1, ...), kind=kOutput, calls=%fused_computation.18 | convolution fusion | flops 127795200 | bytes 3817476 | tf_op jit(solution)/shard_map/dot_general | solution.py:56
  60.3 1.9 %collective-permute-start.7 = (bf16[160,1536]{1,0:T(8,128)(2,1)S(1)}, bf16[160,1536]{1,0:T(8,128)(2,1)}, u32[]{:S(2)}, u32[]{:S(2)}) collective-permute-start(bf16[160,1536]{1,0:T(8,128)(2,1)S(1)} %add_convert_fusion), channel_id=1, source_target_pairs={{0,128},{128,0},{1,129},{129,1},{2,130},{130,2},{3,131},{131,3},{4... | collective-permute-start | bytes 1474568 | tf_op jit(solution)/shard_map/ppermute | solution.py:34
  62.2 0.1 fusion.42
  62.3 0.2 slice_reduce_fusion.1
  62.5 1.2 convolution_convert_fusion.2
  63.7 2.4 %collective-permute-start = (bf16[160,1536]{1,0:T(8,128)(2,1)}, bf16[160,1536]{1,0:T(8,128)(2,1)}, u32[]{:S(2)}, u32[]{:S(2)}) collective-permute-start(bf16[160,1536]{1,0:T(8,128)(2,1)} %convolution_convert_fusion.2), channel_id=1, source_target_pairs={{0,128},{128,0},{1,129},{129,1},{2,130},{130,2},{3,131},{131,3},{4... | collective-permute-start | bytes 1474568 | tf_op jit(solution)/shard_map/ppermute | solution.py:34
  66.1 1.3 %fusion.26 = f32[128,1536]{1,0:T(8,128)S(1)} fusion(bf16[160,1536]{1,0:T(8,128)(2,1)} %collective-permute-done.7, s32[128]{0:T(128)S(1)} %get-tuple-element.10, s32[128]{0:T(128)S(1)} %get-tuple-element.9), kind=kOutput, calls=%fused_computation.42 | convolution fusion | flops 62976000 | bytes 1278976 | tf_op jit(solution)/shard_map/dot_general | solution.py:131
  67.5 0.2 slice_reduce_fusion.3
  67.7 1.1 fusion.7
  68.8 12.0 %all-to-all-start.2 = ((bf16[16,8,1536]{2,1,0:T(8,128)(2,1)}), bf16[16,8,1536]{2,1,0:T(8,128)(2,1)S(1)}, u32[]{:S(2)}, u32[]{:S(2)}) async-start(bf16[16,8,1536]{2,1,0:T(8,128)(2,1)} %fusion.7), calls=%async_computation.2 | async-start | bytes 786432 | tf_op jit(solution)/shard_map/all_to_all | solution.py:16
  80.8 1.4 %fusion.6 = bf16[160,1536]{1,0:T(8,128)(2,1)S(1)} fusion(bf16[160,1536]{1,0:T(8,128)(2,1)} %collective-permute-done, bf16[128,1664]{1,0:T(8,128)(2,1)S(1)} %bitcast.65, s32[128]{0:T(128)S(1)} %get-tuple-element.8, s32[128]{0:T(128)S(1)} %get-tuple-element.7), kind=kOutput, calls=%fused_computation.15 | convolution fusion | flops 63467520 | bytes 1377280 | tf_op jit(solution)/shard_map/dot_general | solution.py:95
  82.2 2.6 %collective-permute-start.3 = (bf16[160,1536]{1,0:T(8,128)(2,1)S(1)}, bf16[160,1536]{1,0:T(8,128)(2,1)S(1)}, u32[]{:S(2)}, u32[]{:S(2)}) collective-permute-start(bf16[160,1536]{1,0:T(8,128)(2,1)S(1)} %fusion.6), channel_id=1, source_target_pairs={{0,16},{8,24},{16,0},{24,8},{1,17},{9,25},{17,1},{25,9},{2,18},{10... | collective-permute-start | bytes 1474568 | tf_op jit(solution)/shard_map/ppermute | solution.py:30
  84.8 1.9 %collective-permute-start.2 = (bf16[160,1536]{1,0:T(8,128)(2,1)S(1)}, bf16[160,1536]{1,0:T(8,128)(2,1)S(1)}, u32[]{:S(2)}, u32[]{:S(2)}) collective-permute-start(bf16[160,1536]{1,0:T(8,128)(2,1)S(1)} %fusion.6), channel_id=1, source_target_pairs={{0,24},{8,0},{16,8},{24,16},{1,25},{9,1},{17,9},{25,17},{2,26},{10... | collective-permute-start | bytes 1474568 | tf_op jit(solution)/shard_map/ppermute | solution.py:30
  86.8 3.9 %collective-permute-start.1 = (bf16[160,1536]{1,0:T(8,128)(2,1)S(1)}, bf16[160,1536]{1,0:T(8,128)(2,1)S(1)}, u32[]{:S(2)}, u32[]{:S(2)}) collective-permute-start(bf16[160,1536]{1,0:T(8,128)(2,1)S(1)} %fusion.6), channel_id=1, source_target_pairs={{0,8},{8,16},{16,24},{24,0},{1,9},{9,17},{17,25},{25,1},{2,10},{10... | collective-permute-start | bytes 1474568 | tf_op jit(solution)/shard_map/ppermute | solution.py:30
  90.7 0.7 pad_maximum_fusion.2
  91.5 8.3 %collective-permute-done.3 = bf16[160,1536]{1,0:T(8,128)(2,1)S(1)} collective-permute-done((bf16[160,1536]{1,0:T(8,128)(2,1)S(1)}, bf16[160,1536]{1,0:T(8,128)(2,1)S(1)}, u32[]{:S(2)}, u32[]{:S(2)}) %collective-permute-start.3) | collective-permute-done | bytes 491552 | tf_op jit(solution)/shard_map/ppermute | solution.py:30
  99.8 6.0 %collective-permute-done.2 = bf16[160,1536]{1,0:T(8,128)(2,1)S(1)} collective-permute-done((bf16[160,1536]{1,0:T(8,128)(2,1)S(1)}, bf16[160,1536]{1,0:T(8,128)(2,1)S(1)}, u32[]{:S(2)}, u32[]{:S(2)}) %collective-permute-start.2) | collective-permute-done | bytes 491552 | tf_op jit(solution)/shard_map/ppermute | solution.py:30
  105.8 2.9 %collective-permute-done.1 = bf16[160,1536]{1,0:T(8,128)(2,1)S(1)} collective-permute-done((bf16[160,1536]{1,0:T(8,128)(2,1)S(1)}, bf16[160,1536]{1,0:T(8,128)(2,1)S(1)}, u32[]{:S(2)}, u32[]{:S(2)}) %collective-permute-start.1) | collective-permute-done | bytes 491552 | tf_op jit(solution)/shard_map/ppermute | solution.py:30
  108.7 0.1 pad_maximum_fusion
  108.9 1.7 %fusion = bf16[1,1536,256]{2,1,0:T(8,128)(2,1)} fusion(bf16[640,1536]{1,0:T(8,128)(2,1)S(1)} %pad_maximum_fusion, bf16[640,256]{1,0:T(8,128)(2,1)S(1)} %pad_maximum_fusion.1), kind=kOutput, calls=%fused_computation.7 | convolution fusion | flops 503709696 | bytes 3080192 | tf_op jit(solution)/shard_map/dot_general | solution.py:122
  110.6 0.1 convert_reduce_fusion
  110.7 0.2 fusion.58
  110.9 0.6 broadcast_in_dim.20
  111.5 4.5 %all-to-all-start.3 = ((f32[4,1,8]{2,1,0:T(1,128)}), f32[4,1,8]{2,1,0:T(1,128)S(1)}, u32[]{:S(2)}, u32[]{:S(2)}) async-start(f32[4,1,8]{2,1,0:T(1,128)} %broadcast_in_dim.20), calls=%async_computation.3 | async-start | bytes 4096 | tf_op jit(solution)/shard_map/all_to_all | solution.py:16
  116.0 2.7 %fusion.1 = bf16[1,1536,256]{2,1,0:T(8,128)(2,1)} fusion(bf16[640,1536]{1,0:T(8,128)(2,1)S(1)} %pad_maximum_fusion, bf16[640,256]{1,0:T(8,128)(2,1)} %pad_maximum_fusion.2), kind=kOutput, calls=%fused_computation.8 | convolution fusion | flops 503709696 | bytes 3080192 | tf_op jit(solution)/shard_map/dot_general | solution.py:125
  118.7 2.5 %all-to-all-done.3 = f32[4,1,8]{2,1,0:T(1,128)S(1)} async-done(((f32[4,1,8]{2,1,0:T(1,128)}), f32[4,1,8]{2,1,0:T(1,128)S(1)}, u32[]{:S(2)}, u32[]{:S(2)}) %all-to-all-start.3) | async-done | bytes 160 | tf_op jit(solution)/shard_map/all_to_all | solution.py:16
  121.2 0.7 fusion.61
  (52 shorter events, 0.2 us)
Async XLA Ops:
  0.6 8.0 %copy-start = (bf16[1,1536,256]{2,1,0:T(8,128)(2,1)S(1)}, bf16[1,1536,256]{2,1,0:T(8,128)(2,1)}, u32[]{:S(2)}) copy-start(bf16[1,1536,256]{2,1,0:T(8,128)(2,1)} %param.12) | copy-start | bytes 2359300
  0.6 8.4 %copy-start.1 = (bf16[1,1536,256]{2,1,0:T(8,128)(2,1)S(1)}, bf16[1,1536,256]{2,1,0:T(8,128)(2,1)}, u32[]{:S(2)}) copy-start(bf16[1,1536,256]{2,1,0:T(8,128)(2,1)} %param.13) | copy-start | bytes 2359300
  2.2 13.3 %all-to-all-start = ((f32[4,1,8]{2,1,0:T(1,128)}), f32[4,1,8]{2,1,0:T(1,128)S(1)}, u32[]{:S(2)}, u32[]{:S(2)}) async-start(f32[4,1,8]{2,1,0:T(1,128)} %broadcast_in_dim.15), calls=%async_computation | async-start | bytes 4096 | tf_op jit(solution)/shard_map/all_to_all | solution.py:16
  8.6 1.7 %copy-start.6 = (bf16[160,256]{1,0:T(8,128)(2,1)}, bf16[160,256]{1,0:T(8,128)(2,1)S(1)}, u32[]{:S(2)}) copy-start(bf16[160,256]{1,0:T(8,128)(2,1)S(1)} %get-tuple-element.15) | copy-start | bytes 245764
  8.6 6.5 %copy-start.2 = (bf16[160,256]{1,0:T(8,128)(2,1)}, bf16[160,256]{1,0:T(8,128)(2,1)S(1)}, u32[]{:S(2)}) copy-start(bf16[160,256]{1,0:T(8,128)(2,1)S(1)} %get-tuple-element.23) | copy-start | bytes 245764
  8.6 23.1 %copy-start.4 = (bf16[160,256]{1,0:T(8,128)(2,1)}, bf16[160,256]{1,0:T(8,128)(2,1)S(1)}, u32[]{:S(2)}) copy-start(bf16[160,256]{1,0:T(8,128)(2,1)S(1)} %get-tuple-element.14) | copy-start | bytes 245764
  8.6 26.6 %copy-start.8 = (bf16[160,256]{1,0:T(8,128)(2,1)}, bf16[160,256]{1,0:T(8,128)(2,1)S(1)}, u32[]{:S(2)}) copy-start(bf16[160,256]{1,0:T(8,128)(2,1)S(1)} %get-tuple-element.16) | copy-start | bytes 245764
  8.6 6.3 %copy-start.17 = (s32[8,2]{0,1:T(2,128)S(1)}, s32[8,2]{0,1:T(2,128)}, u32[]{:S(2)}) copy-start(s32[8,2]{0,1:T(2,128)} %param.10) | copy-start | bytes 196
  8.6 6.4 %copy-start.18 = (s32[8,2]{0,1:T(2,128)S(1)}, s32[8,2]{0,1:T(2,128)}, u32[]{:S(2)}) copy-start(s32[8,2]{0,1:T(2,128)} %param.11) | copy-start | bytes 196
  9.0 6.5 %copy-start.10 = (bf16[8,1536]{1,0:T(8,128)(2,1)S(1)}, bf16[8,1536]{1,0:T(8,128)(2,1)}, u32[]{:S(2)}) copy-start(bf16[8,1536]{1,0:T(8,128)(2,1)} %param.8) | copy-start | bytes 73732
  9.0 6.5 %copy-start.14 = (f32[1536]{0:T(1024)S(1)}, f32[1536]{0:T(1024)}, u32[]{:S(2)}) copy-start(f32[1536]{0:T(1024)} %param.9) | copy-start | bytes 18436
  10.2 30.9 %collective-permute-start.6 = (bf16[160,1536]{1,0:T(8,128)(2,1)}, bf16[160,1536]{1,0:T(8,128)(2,1)}, u32[]{:S(2)}, u32[]{:S(2)}) collective-permute-start(bf16[160,1536]{1,0:T(8,128)(2,1)} %fusion.4), channel_id=1, source_target_pairs={{0,24},{8,0},{16,8},{24,16},{1,25},{9,1},{17,9},{25,17},{2,26},{10... | collective-permute-start | bytes 1474568 | tf_op jit(solution)/shard_map/ppermute | solution.py:30
  15.6 19.6 %copy-start.15 = (f32[8]{0:T(128)}, f32[8]{0:T(128)S(1)}, u32[]{:S(2)}) copy-start(f32[8]{0:T(128)S(1)} %add_rsqrt_fusion) | copy-start | bytes 100
  16.5 45.7 %all-to-all-start.1 = ((bf16[16,8,1664]{2,1,0:T(8,128)(2,1)}), bf16[16,8,1664]{2,1,0:T(8,128)(2,1)S(1)}, u32[]{:S(2)}, u32[]{:S(2)}) async-start(bf16[16,8,1664]{2,1,0:T(8,128)(2,1)} %broadcast_in_dim.16), calls=%async_computation.1 | async-start | bytes 851968 | tf_op jit(solution)/shard_map/all_to_all | solution.py:16
  32.9 25.7 %collective-permute-start.5 = (bf16[160,1536]{1,0:T(8,128)(2,1)}, bf16[160,1536]{1,0:T(8,128)(2,1)S(1)}, u32[]{:S(2)}, u32[]{:S(2)}) collective-permute-start(bf16[160,1536]{1,0:T(8,128)(2,1)} %fusion.3), channel_id=1, source_target_pairs={{0,8},{8,16},{16,24},{24,0},{1,9},{9,17},{17,25},{25,1},{2,10},{10... | collective-permute-start | bytes 1474568 | tf_op jit(solution)/shard_map/ppermute | solution.py:30
  35.6 22.9 %collective-permute-start.4 = (bf16[160,1536]{1,0:T(8,128)(2,1)S(1)}, bf16[160,1536]{1,0:T(8,128)(2,1)}, u32[]{:S(2)}, u32[]{:S(2)}) collective-permute-start(bf16[160,1536]{1,0:T(8,128)(2,1)S(1)} %fusion.2), channel_id=1, source_target_pairs={{0,16},{8,24},{16,0},{24,8},{1,17},{9,25},{17,1},{25,9},{2,18},{10... | collective-permute-start | bytes 1474568 | tf_op jit(solution)/shard_map/ppermute | solution.py:30
  60.3 5.8 %collective-permute-start.7 = (bf16[160,1536]{1,0:T(8,128)(2,1)S(1)}, bf16[160,1536]{1,0:T(8,128)(2,1)}, u32[]{:S(2)}, u32[]{:S(2)}) collective-permute-start(bf16[160,1536]{1,0:T(8,128)(2,1)S(1)} %add_convert_fusion), channel_id=1, source_target_pairs={{0,128},{128,0},{1,129},{129,1},{2,130},{130,2},{3,131},{131,3},{4... | collective-permute-start | bytes 1474568 | tf_op jit(solution)/shard_map/ppermute | solution.py:34
  63.7 17.1 %collective-permute-start = (bf16[160,1536]{1,0:T(8,128)(2,1)}, bf16[160,1536]{1,0:T(8,128)(2,1)}, u32[]{:S(2)}, u32[]{:S(2)}) collective-permute-start(bf16[160,1536]{1,0:T(8,128)(2,1)} %convolution_convert_fusion.2), channel_id=1, source_target_pairs={{0,128},{128,0},{1,129},{129,1},{2,130},{130,2},{3,131},{131,3},{4... | collective-permute-start | bytes 1474568 | tf_op jit(solution)/shard_map/ppermute | solution.py:34
  67.5 23.2 %copy-start.5 = (bf16[160,256]{1,0:T(8,128)(2,1)S(1)}, bf16[160,256]{1,0:T(8,128)(2,1)}, u32[]{:S(2)}) copy-start(bf16[160,256]{1,0:T(8,128)(2,1)} %copy-done.4) | copy-start | bytes 245764
  67.5 23.2 %copy-start.7 = (bf16[160,256]{1,0:T(8,128)(2,1)S(1)}, bf16[160,256]{1,0:T(8,128)(2,1)}, u32[]{:S(2)}) copy-start(bf16[160,256]{1,0:T(8,128)(2,1)} %copy-done.6) | copy-start | bytes 245764
  67.5 23.2 %copy-start.9 = (bf16[160,256]{1,0:T(8,128)(2,1)S(1)}, bf16[160,256]{1,0:T(8,128)(2,1)}, u32[]{:S(2)}) copy-start(bf16[160,256]{1,0:T(8,128)(2,1)} %copy-done.8) | copy-start | bytes 245764
  67.5 23.2 %copy-start.13 = (bf16[160,256]{1,0:T(8,128)(2,1)S(1)}, bf16[160,256]{1,0:T(8,128)(2,1)}, u32[]{:S(2)}) copy-start(bf16[160,256]{1,0:T(8,128)(2,1)} %get-tuple-element.13) | copy-start | bytes 245764
  67.7 23.8 %copy-start.3 = (bf16[160,256]{1,0:T(8,128)(2,1)S(1)}, bf16[160,256]{1,0:T(8,128)(2,1)}, u32[]{:S(2)}) copy-start(bf16[160,256]{1,0:T(8,128)(2,1)} %copy-done.2) | copy-start | bytes 245764
  67.7 23.8 %copy-start.12 = (bf16[160,256]{1,0:T(8,128)(2,1)S(1)}, bf16[160,256]{1,0:T(8,128)(2,1)}, u32[]{:S(2)}) copy-start(bf16[160,256]{1,0:T(8,128)(2,1)} %get-tuple-element.24) | copy-start | bytes 245764
  68.8 41.8 %all-to-all-start.2 = ((bf16[16,8,1536]{2,1,0:T(8,128)(2,1)}), bf16[16,8,1536]{2,1,0:T(8,128)(2,1)S(1)}, u32[]{:S(2)}, u32[]{:S(2)}) async-start(bf16[16,8,1536]{2,1,0:T(8,128)(2,1)} %fusion.7), calls=%async_computation.2 | async-start | bytes 786432 | tf_op jit(solution)/shard_map/all_to_all | solution.py:16
  82.2 17.5 %collective-permute-start.3 = (bf16[160,1536]{1,0:T(8,128)(2,1)S(1)}, bf16[160,1536]{1,0:T(8,128)(2,1)S(1)}, u32[]{:S(2)}, u32[]{:S(2)}) collective-permute-start(bf16[160,1536]{1,0:T(8,128)(2,1)S(1)} %fusion.6), channel_id=1, source_target_pairs={{0,16},{8,24},{16,0},{24,8},{1,17},{9,25},{17,1},{25,9},{2,18},{10... | collective-permute-start | bytes 1474568 | tf_op jit(solution)/shard_map/ppermute | solution.py:30
  84.8 21.0 %collective-permute-start.2 = (bf16[160,1536]{1,0:T(8,128)(2,1)S(1)}, bf16[160,1536]{1,0:T(8,128)(2,1)S(1)}, u32[]{:S(2)}, u32[]{:S(2)}) collective-permute-start(bf16[160,1536]{1,0:T(8,128)(2,1)S(1)} %fusion.6), channel_id=1, source_target_pairs={{0,24},{8,0},{16,8},{24,16},{1,25},{9,1},{17,9},{25,17},{2,26},{10... | collective-permute-start | bytes 1474568 | tf_op jit(solution)/shard_map/ppermute | solution.py:30
  86.8 22.0 %collective-permute-start.1 = (bf16[160,1536]{1,0:T(8,128)(2,1)S(1)}, bf16[160,1536]{1,0:T(8,128)(2,1)S(1)}, u32[]{:S(2)}, u32[]{:S(2)}) collective-permute-start(bf16[160,1536]{1,0:T(8,128)(2,1)S(1)} %fusion.6), channel_id=1, source_target_pairs={{0,8},{8,16},{16,24},{24,0},{1,9},{9,17},{17,25},{25,1},{2,10},{10... | collective-permute-start | bytes 1474568 | tf_op jit(solution)/shard_map/ppermute | solution.py:30
  108.9 1.8 %copy-start.11 = (bf16[8,1536]{1,0:T(8,128)(2,1)S(1)}, bf16[8,1536]{1,0:T(8,128)(2,1)}, u32[]{:S(2)}) copy-start(bf16[8,1536]{1,0:T(8,128)(2,1)} %param.8) | copy-start | bytes 73732
  108.9 1.8 %copy-start.16 = (f32[8]{0:T(128)S(1)}, f32[8]{0:T(128)}, u32[]{:S(2)}) copy-start(f32[8]{0:T(128)} %copy-done.15) | copy-start | bytes 100
  111.5 9.7 %all-to-all-start.3 = ((f32[4,1,8]{2,1,0:T(1,128)}), f32[4,1,8]{2,1,0:T(1,128)S(1)}, u32[]{:S(2)}, u32[]{:S(2)}) async-start(f32[4,1,8]{2,1,0:T(1,128)} %broadcast_in_dim.20), calls=%async_computation.3 | async-start | bytes 4096 | tf_op jit(solution)/shard_map/all_to_all | solution.py:16
